TPU v7x, 32 devices: a whole 2x2x4 slice. The times are simulated.
32 devices in a mesh: blk: 4 (over x, core), heads: 8 (over z, y).
Axes of the slice: x: 2, y: 2, z: 4, core: 2. Of those that a mesh axis runs over, the one named last changes fastest.
Arguments:
- queries: bfloat16 [2048, 8192], P('blk', 'heads'), may hold values from -6 to 6
- key_rows: bfloat16 [2048, 1024], P('blk'), may hold values from -6 to 6
- value_head_rows: bfloat16 [2048, 1024], P('blk'), may hold values from -6 to 6
- out_weight: bfloat16 [8192, 4096], P('heads', 'blk'), may hold values from -0.0625 to 0.0625
Outputs:
- projected: bfloat16 [2048, 4096], P(('blk', 'heads'))
All inputs are finite; a program needn't handle non-finite values.
Results may differ from a plain program's by a relative error of at most 0.013.
Values may be sent and summed in bfloat16 or wider, within the bound.
A program may use at most 64 MiB of HBM per device.

v0:
```python
import math

import jax
import jax.numpy as jnp
from jax import lax
from jax.sharding import PartitionSpec as P

QUERY_HEADS = 64
KEY_VALUE_HEADS = 8
HEAD_SIZE = 128
TOK_DEV = 512


MASKED_SCORE = -1e30


def stacked(segment, per_device):
    amount = segment.shape[0]
    return (
        segment.reshape(amount, per_device, HEAD_SIZE)
        .transpose(1, 0, 2)
        .reshape(per_device * amount, HEAD_SIZE)
    )


def unstacked(segment, per_device):
    amount = segment.shape[0] // per_device
    return (
        segment.reshape(per_device, amount, HEAD_SIZE)
        .transpose(1, 0, 2)
        .reshape(amount, per_device * HEAD_SIZE)
    )


def empty_state(amount):
    return (
        jnp.full((amount,), MASKED_SCORE, jnp.float32),
        jnp.zeros((amount,), jnp.float32),
        jnp.zeros((amount, HEAD_SIZE), jnp.float32),
    )


def fold_block(carried, query_set, query_pos, key_block, value_block, key_pos):
    running_max, totals, accumulated = carried
    inv_root = HEAD_SIZE ** (-0.5)
    scores = (
        jnp.einsum("qd,kd->qk", query_set, key_block, preferred_element_type=jnp.float32) * inv_root
    )
    visible = query_pos[:, None] >= key_pos[None, :]
    masked = jnp.where(visible, scores, MASKED_SCORE)
    new_max = jnp.maximum(running_max, jnp.max(masked, axis=1))
    weights = jnp.where(visible, jnp.exp(masked - new_max[:, None]), 0.0)
    rescale = jnp.exp(running_max - new_max)
    totals = totals * rescale + jnp.sum(weights, axis=1)
    mixed = jnp.dot(weights.astype(jnp.bfloat16), value_block, preferred_element_type=jnp.float32)
    accumulated = accumulated * rescale[:, None] + mixed
    return (new_max, totals, accumulated)


def fold_piece(carried, query_set, query_pos, latest, key_piece, value_piece):
    piece_rows = key_piece.shape[0]
    step_rows = math.gcd(piece_rows, TOK_DEV)
    steps_total = piece_rows // step_rows

    def one_step(step_number, inner):
        offset = step_number * step_rows
        key_block = lax.dynamic_slice_in_dim(key_piece, offset, step_rows, 0)
        value_block = lax.dynamic_slice_in_dim(value_piece, offset, step_rows, 0)
        key_pos = offset + jnp.arange(step_rows, dtype=jnp.int32)
        return lax.cond(
            offset <= latest,
            lambda held: fold_block(held, query_set, query_pos, key_block, value_block, key_pos),
            lambda held: held,
            inner,
        )

    return lax.fori_loop(0, steps_total, one_step, carried)


def attend_all(key_cols, value_cols, query_groups):
    initial = tuple((empty_state(entry[0].shape[0]) for entry in query_groups))
    pieces = (
        lax.all_gather(key_cols, "blk", axis=0, tiled=True),
        lax.all_gather(value_cols, "blk", axis=0, tiled=True),
    )
    return tuple(
        (
            fold_piece(held, entry[0], entry[1], entry[2], pieces[0], pieces[1])
            for held, entry in zip(initial, query_groups)
        )
    )


def finished(carried, per_device):
    result = (carried[2] / carried[1][:, None]).astype(jnp.bfloat16)
    return unstacked(result, per_device)


def shards(queries, key_rows, value_head_rows, out_weight):
    row_count = queries.shape[0]
    per_device = queries.shape[1] // HEAD_SIZE
    group_width = QUERY_HEADS // KEY_VALUE_HEADS
    block_index = lax.axis_index("blk")
    head_index = lax.axis_index("heads")
    kv_head = head_index * per_device // group_width
    key_cols = lax.dynamic_slice_in_dim(key_rows, kv_head * HEAD_SIZE, HEAD_SIZE, 1)
    value_cols = lax.dynamic_slice_in_dim(value_head_rows, kv_head * HEAD_SIZE, HEAD_SIZE, 1)
    offsets = jnp.arange(row_count, dtype=jnp.int32)
    own_pos = block_index * row_count + offsets
    finals = attend_all(
        key_cols,
        value_cols,
        ((stacked(queries, per_device), jnp.tile(own_pos, per_device), own_pos[-1]),),
    )
    attended = finished(finals[0], per_device)
    partial_rows = jnp.dot(
        attended,
        lax.all_gather(out_weight, "blk", axis=1, tiled=True),
        preferred_element_type=jnp.float32,
    )
    projected = lax.psum_scatter(
        partial_rows.astype(jnp.bfloat16), "heads", scatter_dimension=0, tiled=True
    )
    return projected


def solution(mesh):
    in_specs = (P("blk", "heads"), P("blk", None), P("blk", None), P("heads", "blk"))
    out_specs = P(("blk", "heads"), None)
    return jax.shard_map(shards, mesh=mesh, in_specs=in_specs, out_specs=out_specs, check_vma=False)
```

profile of v0, /device:TPU:2, one launch (start us, length us, event | category | flops | bytes accessed | tf_op | source)
XLA Modules:
  0.0 178.5 jit_solution(9250108785224543863)
XLA Ops:
  6.5 0.0 copy-start
  6.5 0.0 all-gather.2.cloned.1.call-start
  6.5 0.7 all-gather.2.cloned.1.call-update
  7.3 0.0 reduce-scatter.2.cloned.1.call-start
  7.3 0.6 slice.3
  7.9 0.9 constant_dynamic-slice_fusion.1
  8.8 0.9 constant_dynamic-slice_fusion
  9.7 7.2 %all_gather.9 = bf16[2048,128]{1,0:T(8,128)(2,1)} all-gather(bf16[512,128]{1,0:T(8,128)(2,1)S(1)} %constant_dynamic-slice_fusion.1), channel_id=1, replica_groups=mesh['blk'=4,'heads'=8] {'blk'}, dimensions={0}, use_global_device_ids=true | all-gather | bytes 655360 | tf_op jit(solution)/shard_map/all_gather | solution.py:83
  17.0 10.7 %all_gather.10 = bf16[2048,128]{1,0:T(8,128)(2,1)} all-gather(bf16[512,128]{1,0:T(8,128)(2,1)S(1)} %constant_dynamic-slice_fusion), channel_id=1, replica_groups=mesh['blk'=4,'heads'=8] {'blk'}, dimensions={0}, use_global_device_ids=true | all-gather | bytes 655360 | tf_op jit(solution)/shard_map/all_gather | solution.py:84
  27.7 0.0 copy-done
  27.7 1.2 copy_bitcast_fusion
  28.9 0.1 broadcast_in_dim.28
  29.1 30.6 %while.18 = (s32[]{:T(128)}, f32[4096]{0:T(1024)S(1)}, f32[4096]{0:T(1024)S(1)}, f32[4096,128]{1,0:T(8,128)S(1)}, s32[]{:T(128)}, /*index=5*/bf16[2048,128]{1,0:...) while((s32[]{:T(128)}, f32[4096]{0:T(1024)S(1)}, ...), condition=%wide.region_5.6_spmd.clone, body=%wide.region_0.5_spmd.clone.sunk | while | flops 1108353536 | bytes 31045948 | solution.py:77
  29.7 9.4 %conditional.3 = ((f32[4096]{0:T(1024)S(1)}, f32[4096]{0:T(1024)S(1)}, f32[4096,128]{1,0:T(8,128)S(1)})) conditional(s32[]{:T(128)} %convert_element_type.27, (f32[4096]{0:T(1024)S(1)}, f32[4096]{0:T(1024)S(1)}, f32[4096,128]{1,0:T(8,128)S(1)}) %tuple.53, (s32[512]{0:T(512)S(1)}, s32[]{:T(128)}, s32[512]{0:T(512)S(1)}, bf16[2048,128]{1,0:T(8,128)(2,1)}, ...), branch_computations={%region_1.1_spmd, %region_2.4_spmd} | conditional | flops 1108353536 | bytes 31043662 | solution.py:70
  29.7 2.6 %fusion.2 = (f32[4096]{0:T(1024)S(1)}, f32[512,4096]{1,0:T(8,128)S(1)}) fusion(s32[4096]{0:T(1024)S(1)} %bitcast.31, s32[512]{0:T(512)S(1)} %broadcast_add_fusion, bf16[4096,128]{1,0:T(8,128)(2,1)} %get-tuple-element.265, bf16[2048,128]{1,0:T(8,128)(2,1)} %get-tuple-element.264, s32[]{:T(128)S(6)} %select_n.27), kind=kOutput, calls=%fused_computation.3 | convolution fusion | flops 545255424 | bytes 9603076 | tf_op jit(solution)/shard_map/while/body/eval_jaxpr/cond/branch_1_fun/qd,kd->qk/dot_general | solution.py:47
  32.4 2.5 %fusion.4 = f32[4096]{0:T(1024)S(1)} fusion(f32[512,4096]{1,0:T(8,128)S(1)} %get-tuple-element.332, f32[4096]{0:T(1024)S(1)} %max.5, s32[4096]{0:T(1024)S(1)} %bitcast.32, s32[512]{0:T(512)S(1)} %broadcast_add_fusion), kind=kLoop, calls=%fused_computation.6 | loop fusion | flops 12578816 | bytes 8439808 | tf_op jit(solution)/shard_map/while/body/eval_jaxpr/cond/branch_1_fun/reduce_sum | solution.py:54
  34.9 4.2 %convolution_add_fusion = f32[4096,128]{1,0:T(8,128)S(1)} fusion(f32[512,4096]{1,0:T(8,128)S(1)} %get-tuple-element.332, f32[4096]{0:T(1024)S(1)} %max.5, s32[4096]{0:T(1024)S(1)} %bitcast.33, s32[512]{0:T(512)S(1)} %broadcast_add_fusion, f32[4096,128]{1,0:T(8,128)S(1)} %get-tuple-element.267, f32[4096]{0:T(1024)S(1)} %get-tuple-element.330, ...), kind=kOutput, calls=%fused_computation.4 | convolution fusion | flops 550502400 | bytes 12765188 | tf_op jit(solution)/shard_map/while/body/eval_jaxpr/cond/branch_1_fun/dot_general | solution.py:55
  39.7 9.4 %conditional.3 = ((f32[4096]{0:T(1024)S(1)}, f32[4096]{0:T(1024)S(1)}, f32[4096,128]{1,0:T(8,128)S(1)})) conditional(s32[]{:T(128)} %convert_element_type.27, (f32[4096]{0:T(1024)S(1)}, f32[4096]{0:T(1024)S(1)}, f32[4096,128]{1,0:T(8,128)S(1)}) %tuple.53, (s32[512]{0:T(512)S(1)}, s32[]{:T(128)}, s32[512]{0:T(512)S(1)}, bf16[2048,128]{1,0:T(8,128)(2,1)}, ...), branch_computations={%region_1.1_spmd, %region_2.4_spmd} | conditional | flops 1108353536 | bytes 31043662 | solution.py:70
  39.7 2.6 %fusion.2 = (f32[4096]{0:T(1024)S(1)}, f32[512,4096]{1,0:T(8,128)S(1)}) fusion(s32[4096]{0:T(1024)S(1)} %bitcast.31, s32[512]{0:T(512)S(1)} %broadcast_add_fusion, bf16[4096,128]{1,0:T(8,128)(2,1)} %get-tuple-element.265, bf16[2048,128]{1,0:T(8,128)(2,1)} %get-tuple-element.264, s32[]{:T(128)S(6)} %select_n.27), kind=kOutput, calls=%fused_computation.3 | convolution fusion | flops 545255424 | bytes 9603076 | tf_op jit(solution)/shard_map/while/body/eval_jaxpr/cond/branch_1_fun/qd,kd->qk/dot_general | solution.py:47
  42.4 2.5 %fusion.4 = f32[4096]{0:T(1024)S(1)} fusion(f32[512,4096]{1,0:T(8,128)S(1)} %get-tuple-element.332, f32[4096]{0:T(1024)S(1)} %max.5, s32[4096]{0:T(1024)S(1)} %bitcast.32, s32[512]{0:T(512)S(1)} %broadcast_add_fusion), kind=kLoop, calls=%fused_computation.6 | loop fusion | flops 12578816 | bytes 8439808 | tf_op jit(solution)/shard_map/while/body/eval_jaxpr/cond/branch_1_fun/reduce_sum | solution.py:54
  44.9 4.2 %convolution_add_fusion = f32[4096,128]{1,0:T(8,128)S(1)} fusion(f32[512,4096]{1,0:T(8,128)S(1)} %get-tuple-element.332, f32[4096]{0:T(1024)S(1)} %max.5, s32[4096]{0:T(1024)S(1)} %bitcast.33, s32[512]{0:T(512)S(1)} %broadcast_add_fusion, f32[4096,128]{1,0:T(8,128)S(1)} %get-tuple-element.267, f32[4096]{0:T(1024)S(1)} %get-tuple-element.330, ...), kind=kOutput, calls=%fused_computation.4 | convolution fusion | flops 550502400 | bytes 12765188 | tf_op jit(solution)/shard_map/while/body/eval_jaxpr/cond/branch_1_fun/dot_general | solution.py:55
  49.7 9.4 %conditional.3 = ((f32[4096]{0:T(1024)S(1)}, f32[4096]{0:T(1024)S(1)}, f32[4096,128]{1,0:T(8,128)S(1)})) conditional(s32[]{:T(128)} %convert_element_type.27, (f32[4096]{0:T(1024)S(1)}, f32[4096]{0:T(1024)S(1)}, f32[4096,128]{1,0:T(8,128)S(1)}) %tuple.53, (s32[512]{0:T(512)S(1)}, s32[]{:T(128)}, s32[512]{0:T(512)S(1)}, bf16[2048,128]{1,0:T(8,128)(2,1)}, ...), branch_computations={%region_1.1_spmd, %region_2.4_spmd} | conditional | flops 1108353536 | bytes 31043662 | solution.py:70
  49.7 2.6 %fusion.2 = (f32[4096]{0:T(1024)S(1)}, f32[512,4096]{1,0:T(8,128)S(1)}) fusion(s32[4096]{0:T(1024)S(1)} %bitcast.31, s32[512]{0:T(512)S(1)} %broadcast_add_fusion, bf16[4096,128]{1,0:T(8,128)(2,1)} %get-tuple-element.265, bf16[2048,128]{1,0:T(8,128)(2,1)} %get-tuple-element.264, s32[]{:T(128)S(6)} %select_n.27), kind=kOutput, calls=%fused_computation.3 | convolution fusion | flops 545255424 | bytes 9603076 | tf_op jit(solution)/shard_map/while/body/eval_jaxpr/cond/branch_1_fun/qd,kd->qk/dot_general | solution.py:47
  52.4 2.5 %fusion.4 = f32[4096]{0:T(1024)S(1)} fusion(f32[512,4096]{1,0:T(8,128)S(1)} %get-tuple-element.332, f32[4096]{0:T(1024)S(1)} %max.5, s32[4096]{0:T(1024)S(1)} %bitcast.32, s32[512]{0:T(512)S(1)} %broadcast_add_fusion), kind=kLoop, calls=%fused_computation.6 | loop fusion | flops 12578816 | bytes 8439808 | tf_op jit(solution)/shard_map/while/body/eval_jaxpr/cond/branch_1_fun/reduce_sum | solution.py:54
  54.9 4.2 %convolution_add_fusion = f32[4096,128]{1,0:T(8,128)S(1)} fusion(f32[512,4096]{1,0:T(8,128)S(1)} %get-tuple-element.332, f32[4096]{0:T(1024)S(1)} %max.5, s32[4096]{0:T(1024)S(1)} %bitcast.33, s32[512]{0:T(512)S(1)} %broadcast_add_fusion, f32[4096,128]{1,0:T(8,128)S(1)} %get-tuple-element.267, f32[4096]{0:T(1024)S(1)} %get-tuple-element.330, ...), kind=kOutput, calls=%fused_computation.4 | convolution fusion | flops 550502400 | bytes 12765188 | tf_op jit(solution)/shard_map/while/body/eval_jaxpr/cond/branch_1_fun/dot_general | solution.py:55
  59.7 1.6 divide_convert_fusion
  61.3 1.5 copy.8
  62.8 7.3 %all-gather.2.cloned.1.call-done = bf16[1024,4096]{1,0:T(8,128)(2,1)} async-done(((bf16[1024,1024]{1,0:T(8,128)(2,1)}), bf16[1024,4096]{1,0:T(8,128)(2,1)}) %all-gather.2.cloned.1.call-update) | async-done | bytes 8388624 | tf_op jit(solution)/shard_map/all_gather | solution.py:118
  70.1 9.5 %convolution_convert_fusion = bf16[512,4096]{1,0:T(8,128)(2,1)} fusion(bf16[512,1024]{0,1:T(8,128)(2,1)S(1)} %bitcast.35, bf16[1024,4096]{1,0:T(8,128)(2,1)} %all-gather.2.cloned.1.call-done), kind=kOutput, calls=%fused_computation.25 | convolution fusion | flops 4297064448 | bytes 13631488 | tf_op jit(solution)/shard_map/dot_general | solution.py:116
  79.6 0.0 reduce-scatter.2.cloned.1.call-update
  79.6 92.1 %reduce-scatter.2.cloned.1.call-done = bf16[64,4096]{1,0:T(8,128)(2,1)} async-done(((bf16[512,4096]{1,0:T(8,128)(2,1)}), bf16[64,4096]{1,0:T(8,128)(2,1)}) %reduce-scatter.2.cloned.1.call-update) | async-done | bytes 524304 | tf_op jit(solution)/shard_map/reduce_scatter | solution.py:121
  (26 shorter events, 0.1 us)
Async XLA Ops:
  6.5 21.1 %copy-start = (bf16[512,1024]{1,0:T(8,128)(2,1)S(1)}, bf16[512,1024]{1,0:T(8,128)(2,1)}, u32[]{:S(2)}) copy-start(bf16[512,1024]{1,0:T(8,128)(2,1)} %param.8) | copy-start | bytes 3145732
  6.5 63.6 %all-gather.2.cloned.1.call-start = ((), (), s32[]{:S(2)}) async-start(), calls=%async_computation.1 | async-start | bytes 10485760 | tf_op jit(solution)/shard_map/all_gather | solution.py:118
  7.3 164.4 %reduce-scatter.2.cloned.1.call-start = ((), (), s32[]{:S(2)}) async-start(), calls=%async_computation.2 | async-start | bytes 4718592 | tf_op jit(solution)/shard_map/reduce_scatter | solution.py:121
Sparse Core Ops, SparseCore 0:
  8.9 61.1 all-gather.1
  79.7 91.9 reduce-scatter.1
where the time goes:
time: 180 us; the launch traced here: 179 us
  waiting for transfers between devices  100 us (56%)
  matrix products  30 us (17%)
  blocking collectives  17.9 us (10%)
  between operations  13.4 us (7%)
  other arithmetic  9 us (5%)
  local copies, waits for them, and re-layouts  5.32 us (3%)
  loops' own time  2.67 us (1%)
    reduce_scatter x1, waiting for transfers between devices, shards(): lax.psum_scatter(partial_rows.astype(jnp.bfloat16), 'heads', scatter_dime...  92.1 us
    dot_general x3, matrix products, fold_block(): jnp.dot(weights.astype(jnp.bfloat16), value_block, preferred_element_type...  12.6 us
    all_gather x1, blocking collectives, attend_all(): lax.all_gather(value_cols, 'blk', axis=0, tiled=True)  10.7 us
    dot_general x1, matrix products, shards(): jnp.dot(attended, lax.all_gather(out_weight, 'blk', axis=1, tiled=True),...  9.48 us
    dot_general x3, matrix products, fold_block(): jnp.einsum('qd,kd->qk', query_set, key_block, preferred_element_type=jnp....  7.88 us
    reduce_sum x3, other arithmetic, fold_block(): totals = totals * rescale + jnp.sum(weights, axis=1)  7.38 us
    all_gather x1, waiting for transfers between devices, shards(): lax.all_gather(out_weight, 'blk', axis=1, tiled=True)  7.34 us
    all_gather x1, blocking collectives, attend_all(): lax.all_gather(key_cols, 'blk', axis=0, tiled=True)  7.21 us
  transfers between devices with their start and end apart: 2, of which 2 were waited for; matrix products, arithmetic and copies ran while one was open for 19% of the time, Pallas kernels for 0%

commit v1 on v0

v1 whole, which is shorter than its diff:
```python
import functools
import math

import jax
import jax.numpy as jnp
from jax import lax
from jax.experimental import pallas as pl
from jax.experimental.pallas import tpu as pltpu
from jax.sharding import PartitionSpec as P

QUERY_HEADS = 64
KEY_VALUE_HEADS = 8
HEAD_SIZE = 128
MASKED_SCORE = -1e30
COLUMN_STEP = 256
F32 = jnp.float32
BF16 = jnp.bfloat16


def kernel(nb, nh, q_ref, k_ref, v_ref, w_ref, out_ref,
           kbuf, vbuf, wbuf, acc, top, att, ysend, yrecv, zsend, zrecv,
           local_sem, kv_send, kv_recv, relay_send, w_send, w_recv,
           att_send, att_recv, y_send, y_recv, z_send, z_recv):
    nx, nz = nb // 2, nh // 2
    rows = k_ref.shape[0]
    piece = rows // nh
    half = rows // 2
    heads = q_ref.shape[3] // HEAD_SIZE
    depth, wcols = w_ref.shape
    step = wbuf.shape[3]
    ns = wcols // step
    scale = math.log2(math.e) * HEAD_SIZE ** (-0.5)

    b, h = lax.axis_index("blk"), lax.axis_index("heads")
    x, c = b // 2, b % 2
    z, y = h // 2, h % 2
    partner = x * 2 + (1 - c)
    kv_col = pl.multiple_of((h * heads // (QUERY_HEADS // KEY_VALUE_HEADS)) * HEAD_SIZE, HEAD_SIZE)

    def remote(src, dst, ssem, rsem, blk, hd):
        return pltpu.make_async_remote_copy(
            src_ref=src, dst_ref=dst, send_sem=ssem, recv_sem=rsem,
            device_id=(blk, hd), device_id_type=pl.DeviceIdType.MESH)

    k_own = k_ref.at[:, pl.ds(kv_col, HEAD_SIZE)]
    v_own = v_ref.at[:, pl.ds(kv_col, HEAD_SIZE)]
    local_k = pltpu.make_async_copy(k_own, kbuf.at[b], local_sem.at[0])
    local_v = pltpu.make_async_copy(v_own, vbuf.at[b], local_sem.at[1])
    local_k.start()
    local_v.start()

    def w_cols(s):
        return w_ref.at[:, pl.ds(s * step, step)]

    local_w = [pltpu.make_async_copy(w_cols(s), wbuf.at[x, s], local_sem.at[2 + s]) for s in range(ns)]
    for copy in local_w:
        copy.start()

    barrier = pltpu.get_barrier_semaphore()

    def greet(blk, hd):
        pl.semaphore_signal(barrier, inc=1, device_id=(blk, hd), device_id_type=pl.DeviceIdType.MESH)

    for i in range(1, nx):
        greet(lax.rem(x + i, nx) * 2 + c, h)
    greet(b, z * 2 + (1 - y))

    def greet_owner(d, carry):
        @pl.when(d != c * nz + z)
        def _():
            greet(x * 2 + d // nz, (d % nz) * 2 + y)
        return carry

    lax.fori_loop(0, 2 * nz, greet_owner, 0)
    pl.semaphore_wait(barrier, nx - 1 + 1 + 2 * nz - 1)

    def kv_copy(buf, own, n, src_blk, dst_blk, ssem):
        return remote(own, buf.at[src_blk], ssem, kv_recv.at[n, src_blk], dst_blk, h)

    @pl.when(c == 0)
    def _():
        for n, (buf, own) in enumerate(((kbuf, k_own), (vbuf, v_own))):
            kv_copy(buf, own, n, b, partner, kv_send.at[n, nx]).start()

    for j in range(1, nx):
        @pl.when(j > x)
        def _():
            for n, (buf, own) in enumerate(((kbuf, k_own), (vbuf, v_own))):
                kv_copy(buf, own, n, b, j * 2 + c, kv_send.at[n, j]).start()

    for s in range(ns):
        for i in range(1, nx):
            to = lax.rem(x + i, nx)
            remote(w_cols(s), wbuf.at[x, s], w_send.at[i, s], w_recv.at[x, s], to * 2 + c, h).start()

    def group_y(g):
        return (1 - y) if g == 0 else y

    def scores_of(g, hd, j):
        cols = pl.ds(pl.multiple_of(hd * HEAD_SIZE, HEAD_SIZE), HEAD_SIZE)
        q = q_ref[:, group_y(g), :, cols].reshape(half, HEAD_SIZE)
        s = lax.dot_general(q, kbuf[j], (((1,), (1,)), ((), ())), preferred_element_type=F32)
        return s * scale

    def mixed_of(p, j):
        v = jnp.concatenate([vbuf[j], jnp.ones((rows, HEAD_SIZE), BF16)], axis=1)
        return jnp.dot(p.astype(BF16), v, preferred_element_type=F32)

    def own_block(g):
        row = lax.broadcasted_iota(jnp.int32, (half, rows), 0)
        position = (row // piece * 2 + group_y(g)) * piece + row % piece
        visible = position >= lax.broadcasted_iota(jnp.int32, (half, rows), 1)

        def one(hd, carry):
            s = jnp.where(visible, scores_of(g, hd, b), MASKED_SCORE)
            m = jnp.max(s, axis=1, keepdims=True)
            acc[g, hd] = mixed_of(jnp.exp2(s - m), b)
            top[g, hd] = jnp.broadcast_to(m, (half, HEAD_SIZE))
            return carry

        lax.fori_loop(0, heads, one, 0, unroll=2)

    def other_block(g, j):
        def one(hd, carry):
            s = scores_of(g, hd, j)
            old = top[g, hd][:, :1]
            m = jnp.maximum(old, jnp.max(s, axis=1, keepdims=True))
            acc[g, hd] = acc[g, hd] * jnp.exp2(old - m) + mixed_of(jnp.exp2(s - m), j)
            top[g, hd] = jnp.broadcast_to(m, (half, HEAD_SIZE))
            return carry

        lax.fori_loop(0, heads, one, 0, unroll=2)

    mine = pl.ds(pl.multiple_of(c * half, half), half)
    theirs = pl.ds(pl.multiple_of((1 - c) * half, half), half)

    def att_copy(g, where):
        return remote(att.at[g, where], att.at[g, where], att_send.at[g], att_recv.at[g], partner, h)

    def finish(g):
        def one(hd, carry):
            cols = pl.ds(pl.multiple_of(hd * HEAD_SIZE, HEAD_SIZE), HEAD_SIZE)
            a = acc[g, hd]
            att[g, mine, cols] = (a[:, :HEAD_SIZE] / a[:, HEAD_SIZE:]).astype(BF16)
            return carry

        lax.fori_loop(0, heads, one, 0)
        att_copy(g, mine).start()

    def others(g):
        @pl.when(c == 1)
        def _():
            other_block(g, b - 1)

        def one(j, carry):
            other_block(g, j)
            return carry

        lax.fori_loop(0, 2 * x, one, 0)

    local_k.wait()
    local_v.wait()
    own_block(0)
    own_block(1)

    @pl.when(c == 1)
    def _():
        for n, (buf, own) in enumerate(((kbuf, k_own), (vbuf, v_own))):
            kv_copy(buf, own, n, b - 1, partner, kv_send.at[n, nx]).wait_recv()

    for j in range(nx - 1):
        @pl.when(j < x)
        def _():
            for n, (buf, own) in enumerate(((kbuf, k_own), (vbuf, v_own))):
                at = j * 2 + c
                kv_copy(buf, own, n, at, partner, kv_send.at[n, 0]).wait_recv()
                kv_copy(buf, buf.at[at], n, at, partner, relay_send.at[n, j]).start()

    for j in range(nx - 1):
        @pl.when(j < x)
        def _():
            for n, (buf, own) in enumerate(((kbuf, k_own), (vbuf, v_own))):
                kv_copy(buf, own, n, j * 2 + 1 - c, partner, kv_send.at[n, 0]).wait_recv()

    others(0)
    finish(0)

    chunks = [(i, s) for i in range(nx) for s in range(ns)]

    def from_chip(i):
        return x if i == 0 else lax.rem(x + nx - i, nx)

    def y_copy(k):
        return remote(ysend.at[k], yrecv.at[k], y_send.at[k], y_recv.at[k], b, z * 2 + (1 - y))

    def first(k):
        i, s = chunks[k]
        if i == 0:
            local_w[s].wait()
        else:
            remote(w_cols(s), wbuf.at[from_chip(i), s], w_send.at[i, s], w_recv.at[from_chip(i), s], partner, h).wait_recv()
        d = jnp.dot(att[0], wbuf[from_chip(i), s], preferred_element_type=F32)
        ysend[k] = d.astype(BF16)
        y_copy(k).start()

    def z_copy(k, d, src_z, src_c):
        return remote(zsend.at[k, d], zrecv.at[k, src_c * nz + src_z], z_send.at[k, d],
                      z_recv.at[k, src_c * nz + src_z], x * 2 + d // nz, (d % nz) * 2 + y)

    seat = c * nz + z

    def second(k):
        i, s = chunks[k]
        d = jnp.dot(att[1], wbuf[from_chip(i), s], preferred_element_type=F32)
        y_copy(k).wait_recv()
        d = (d + yrecv[k].astype(F32)).astype(BF16)
        zsend[k] = d.reshape(2 * nz, piece, step)

        def push(t, carry):
            to = lax.rem(seat + t, 2 * nz)
            z_copy(k, to, z, c).start()
            return carry

        lax.fori_loop(1, 2 * nz, push, 0)
        zrecv[k, seat] = zsend[k, seat]

    att_copy(0, theirs).wait_recv()
    for k in range(ns):
        first(k)
    others(1)
    finish(1)
    done = 0
    for k in range(ns, len(chunks)):
        first(k)
        if done == 0:
            att_copy(1, theirs).wait_recv()
        while done < k:
            second(done)
            done += 1
    if done == 0:
        att_copy(1, theirs).wait_recv()
    while done < len(chunks):
        second(done)
        done += 1

    for k, (i, s) in enumerate(chunks):
        def landed(t, carry):
            src = lax.rem(seat + t, 2 * nz)
            z_copy(k, src, src % nz, src // nz).wait_recv()
            return carry

        lax.fori_loop(1, 2 * nz, landed, 0)
        for src_c in range(2):
            total = zrecv[k, src_c * nz].astype(F32)
            for src_z in range(1, nz):
                total += zrecv[k, src_c * nz + src_z].astype(F32)
            col = pl.multiple_of((from_chip(i) * 2 + src_c) * wcols + s * step, step)
            out_ref[:, pl.ds(col, step)] = total.astype(BF16)

    @pl.when(c == 0)
    def _():
        for n, (buf, own) in enumerate(((kbuf, k_own), (vbuf, v_own))):
            kv_copy(buf, own, n, b, partner, kv_send.at[n, nx]).wait_send()

    for j in range(1, nx):
        @pl.when(j > x)
        def _():
            for n, (buf, own) in enumerate(((kbuf, k_own), (vbuf, v_own))):
                kv_copy(buf, own, n, b, j * 2 + c, kv_send.at[n, j]).wait_send()

    for j in range(nx - 1):
        @pl.when(j < x)
        def _():
            for n, (buf, own) in enumerate(((kbuf, k_own), (vbuf, v_own))):
                at = j * 2 + c
                kv_copy(buf, buf.at[at], n, at, partner, relay_send.at[n, j]).wait_send()

    for s in range(ns):
        for i in range(1, nx):
            remote(w_cols(s), wbuf.at[x, s], w_send.at[i, s], w_recv.at[x, s], partner, h).wait_send()
    for g in range(2):
        att_copy(g, mine).wait_send()
    for k in range(len(chunks)):
        y_copy(k).wait_send()

        def left(t, carry):
            z_copy(k, lax.rem(seat + t, 2 * nz), z, c).wait_send()
            return carry

        lax.fori_loop(1, 2 * nz, left, 0)


def shards(nb, nh, queries, key_rows, value_head_rows, out_weight):
    rows, qcols = queries.shape
    depth, wcols = out_weight.shape
    heads = qcols // HEAD_SIZE
    nx, nz = nb // 2, nh // 2
    piece, half = rows // nh, rows // 2
    step = math.gcd(wcols, COLUMN_STEP)
    ns = wcols // step
    nk = nx * ns
    q = queries.reshape(nz, 2, piece, qcols)
    dma = pltpu.SemaphoreType.DMA
    vmem = pl.BlockSpec(memory_space=pltpu.VMEM)
    hbm = pl.BlockSpec(memory_space=pl.ANY)
    return pl.pallas_call(
        functools.partial(kernel, nb, nh),
        out_shape=jax.ShapeDtypeStruct((piece, wcols * nb), BF16),
        in_specs=[vmem, hbm, hbm, hbm],
        out_specs=vmem,
        scratch_shapes=[
            pltpu.VMEM((nb, rows, HEAD_SIZE), BF16),
            pltpu.VMEM((nb, rows, HEAD_SIZE), BF16),
            pltpu.VMEM((nx, ns, depth, step), BF16),
            pltpu.VMEM((2, heads, half, 2 * HEAD_SIZE), F32),
            pltpu.VMEM((2, heads, half, HEAD_SIZE), F32),
            pltpu.VMEM((2, 2 * half, qcols), BF16),
            pltpu.VMEM((nk, 2 * half, step), BF16),
            pltpu.VMEM((nk, 2 * half, step), BF16),
            pltpu.VMEM((nk, 2 * nz, piece, step), BF16),
            pltpu.VMEM((nk, 2 * nz, piece, step), BF16),
            dma((2 + ns,)),
            dma((2, nx + 1)),
            dma((2, nb)),
            dma((2, nx)),
            dma((nx, ns)),
            dma((nx, ns)),
            dma((2,)),
            dma((2,)),
            dma((nk,)),
            dma((nk,)),
            dma((nk, 2 * nz)),
            dma((nk, 2 * nz)),
        ],
        compiler_params=pltpu.CompilerParams(
            collective_id=0, has_side_effects=True, vmem_limit_bytes=50 * 2**20),
    )(q, key_rows, value_head_rows, out_weight)


def solution(mesh):
    in_specs = (P("blk", "heads"), P("blk", None), P("blk", None), P("heads", "blk"))
    out_specs = P(("blk", "heads"), None)
    body = functools.partial(shards, mesh.shape["blk"], mesh.shape["heads"])
    return jax.shard_map(body, mesh=mesh, in_specs=in_specs, out_specs=out_specs, check_vma=False)
```

time: 180 us -> 92.8 us (0.52)
  waiting for transfers between devices: 100 us -> 0 us
  Pallas kernels: 0 us -> 88.1 us
  matrix products: 30 us -> 0 us
  blocking collectives: 17.9 us -> 0 us
  between operations: 13.4 us -> 0.01 us
  other arithmetic: 9 us -> 0 us
  loops' own time: 2.67 us -> 0 us
    reduce_scatter x1 -> x0, waiting for transfers between devices: 92.1 us -> none  [shards(): lax.psum_scatter(partial_rows.astype(jnp.bfloat16), 'heads', scatter_dime...]
    pallas_call x0 -> x1, Pallas kernels: none -> 88.1 us  [shards(): pl.pallas_call(functools.partial(kernel, nb, nh), out_shape=jax.ShapeDtyp...]
    dot_general x7 -> x0, matrix products: 30 us -> none  [the longest x3 12.6 us: fold_block(): jnp.dot(weights.astype(jnp.bfloat16), value_block, preferred_element_type...]
    all_gather x2 -> x0, blocking collectives: 17.9 us -> none  [the longest x1 10.7 us: attend_all(): lax.all_gather(value_cols, 'blk', axis=0, tiled=True)]
    reduce_sum x3 -> x0, other arithmetic: 7.38 us -> none  [fold_block(): totals = totals * rescale + jnp.sum(weights, axis=1)]
    all_gather x1 -> x0, waiting for transfers between devices: 7.34 us -> none  [shards(): lax.all_gather(out_weight, 'blk', axis=1, tiled=True)]
    unnamed x2 -> x7, local copies, waits for them, and re-layouts: 0.01 us -> 4.47 us
    another operation x5 -> x0, loops' own time: 2.67 us -> none  [the longest x1 2.38 us: fold_piece(): return lax.fori_loop(0, steps_total, one_step, carried)]
  transfers between devices with their start and end apart: 2 -> 0, of which waited for: 2 -> 0; matrix products, arithmetic and copies ran while one was open for 19% -> 0% of each run, Pallas kernels for 0% -> 0%
where the time goes in v1:
time: 92.8 us; the launch traced here: 92.6 us
  Pallas kernels  88.1 us (95%)
  local copies, waits for them, and re-layouts  4.47 us (5%)
    pallas_call x1, Pallas kernels, shards(): pl.pallas_call(functools.partial(kernel, nb, nh), out_shape=jax.ShapeDtyp...  88.1 us
    unnamed x7, local copies, waits for them, and re-layouts  4.47 us

profile of v1, /device:TPU:2, one launch (start us, length us, event | category | flops | bytes accessed | tf_op | source)
XLA Modules:
  0.0 92.6 jit_solution(17569037931769071062)
XLA Ops:
  0.0 0.0 copy-start
  0.0 1.2 %copy-done = bf16[512,1024]{1,0:T(8,128)(2,1)S(1)} copy-done((bf16[512,1024]{1,0:T(8,128)(2,1)S(1)}, bf16[512,1024]{1,0:T(8,128)(2,1)}, u32[]{:S(2)}) %copy-start) | copy-done | bytes 1048600
  1.2 0.0 copy-start.1
  1.2 1.2 %copy-done.1 = bf16[512,1024]{1,0:T(8,128)(2,1)S(1)} copy-done((bf16[512,1024]{1,0:T(8,128)(2,1)S(1)}, bf16[512,1024]{1,0:T(8,128)(2,1)}, u32[]{:S(2)}) %copy-start.1) | copy-done | bytes 1048600
  2.5 0.0 copy-start.2
  2.5 1.2 %copy-done.2 = bf16[512,1024]{1,0:T(8,128)(2,1)S(1)} copy-done((bf16[512,1024]{1,0:T(8,128)(2,1)S(1)}, bf16[512,1024]{1,0:T(8,128)(2,1)}, u32[]{:S(2)}) %copy-start.2) | copy-done | bytes 1048600
  3.7 88.1 %shard_map.46 = bf16[64,4096]{1,0:T(8,128)(2,1)S(1)} custom-call(bf16[4,2,64,1024]{3,2,1,0:T(8,128)(2,1)S(1)} %bitcast.1, bf16[512,1024]{1,0:T(8,128)(2,1)S(1)} %copy-done.1, bf16[512,1024]{1,0:T(8,128)(2,1)S(1)} %copy-done.2, bf16[1024,1024]{1,0:T(8,128)(2,1)} %w_ref.1), custom_call_target="tpu_custom_call" | custom-call | tf_op jit(solution)/shard_map/pallas_call | solution.py:306
  91.8 0.8 copy.6
Async XLA Ops:
  0.0 1.2 %copy-start = (bf16[512,1024]{1,0:T(8,128)(2,1)S(1)}, bf16[512,1024]{1,0:T(8,128)(2,1)}, u32[]{:S(2)}) copy-start(bf16[512,1024]{1,0:T(8,128)(2,1)} %param.4) | copy-start | bytes 3145732
  1.2 1.2 %copy-start.1 = (bf16[512,1024]{1,0:T(8,128)(2,1)S(1)}, bf16[512,1024]{1,0:T(8,128)(2,1)}, u32[]{:S(2)}) copy-start(bf16[512,1024]{1,0:T(8,128)(2,1)} %k_ref.1) | copy-start | bytes 3145732
  2.5 1.2 %copy-start.2 = (bf16[512,1024]{1,0:T(8,128)(2,1)S(1)}, bf16[512,1024]{1,0:T(8,128)(2,1)}, u32[]{:S(2)}) copy-start(bf16[512,1024]{1,0:T(8,128)(2,1)} %v_ref.1) | copy-start | bytes 3145732

commit v2 on v1

--- a/solution.py
+++ b/solution.py
@@ -13,12 +13,13 @@
 HEAD_SIZE = 128
 MASKED_SCORE = -1e30
 COLUMN_STEP = 256
+TOTAL_ROWS = 16
 F32 = jnp.float32
 BF16 = jnp.bfloat16
 
 
-def kernel(nb, nh, q_ref, k_ref, v_ref, w_ref, out_ref,
-           kbuf, vbuf, wbuf, acc, top, att, ysend, yrecv, zsend, zrecv,
+def kernel(nb, nh, q_hbm, k_ref, v_ref, w_ref, out_ref,
+           q_ref, kbuf, vbuf, vturn, wbuf, acc, top, att, ysend, yrecv, zsend, zrecv,
            local_sem, kv_send, kv_recv, relay_send, w_send, w_recv,
            att_send, att_recv, y_send, y_recv, z_send, z_recv):
     nx, nz = nb // 2, nh // 2
@@ -46,8 +47,10 @@
     v_own = v_ref.at[:, pl.ds(kv_col, HEAD_SIZE)]
     local_k = pltpu.make_async_copy(k_own, kbuf.at[b], local_sem.at[0])
     local_v = pltpu.make_async_copy(v_own, vbuf.at[b], local_sem.at[1])
+    local_q = pltpu.make_async_copy(q_hbm, q_ref, local_sem.at[2 + ns])
     local_k.start()
     local_v.start()
+    local_q.start()
 
     def w_cols(s):
         return w_ref.at[:, pl.ds(s * step, step)]
@@ -99,23 +102,26 @@
     def scores_of(g, hd, j):
         cols = pl.ds(pl.multiple_of(hd * HEAD_SIZE, HEAD_SIZE), HEAD_SIZE)
         q = q_ref[:, group_y(g), :, cols].reshape(half, HEAD_SIZE)
-        s = lax.dot_general(q, kbuf[j], (((1,), (1,)), ((), ())), preferred_element_type=F32)
+        s = lax.dot_general(kbuf[j], q, (((1,), (1,)), ((), ())), preferred_element_type=F32)
         return s * scale
 
+    def turn(j):
+        vturn[j, :HEAD_SIZE] = vbuf[j].T
+        vturn[j, HEAD_SIZE:] = jnp.ones((TOTAL_ROWS, rows), BF16)
+
     def mixed_of(p, j):
-        v = jnp.concatenate([vbuf[j], jnp.ones((rows, HEAD_SIZE), BF16)], axis=1)
-        return jnp.dot(p.astype(BF16), v, preferred_element_type=F32)
+        return jnp.dot(vturn[j], p.astype(BF16), preferred_element_type=F32)
 
     def own_block(g):
-        row = lax.broadcasted_iota(jnp.int32, (half, rows), 0)
+        row = lax.broadcasted_iota(jnp.int32, (rows, half), 1)
         position = (row // piece * 2 + group_y(g)) * piece + row % piece
-        visible = position >= lax.broadcasted_iota(jnp.int32, (half, rows), 1)
+        visible = position >= lax.broadcasted_iota(jnp.int32, (rows, half), 0)
 
         def one(hd, carry):
             s = jnp.where(visible, scores_of(g, hd, b), MASKED_SCORE)
-            m = jnp.max(s, axis=1, keepdims=True)
+            m = jnp.max(s, axis=0, keepdims=True)
             acc[g, hd] = mixed_of(jnp.exp2(s - m), b)
-            top[g, hd] = jnp.broadcast_to(m, (half, HEAD_SIZE))
+            top[g, hd] = jnp.broadcast_to(m, (8, half))
             return carry
 
         lax.fori_loop(0, heads, one, 0, unroll=2)
@@ -123,10 +129,10 @@
     def other_block(g, j):
         def one(hd, carry):
             s = scores_of(g, hd, j)
-            old = top[g, hd][:, :1]
-            m = jnp.maximum(old, jnp.max(s, axis=1, keepdims=True))
+            old = top[g, hd][:1]
+            m = jnp.maximum(old, jnp.max(s, axis=0, keepdims=True))
             acc[g, hd] = acc[g, hd] * jnp.exp2(old - m) + mixed_of(jnp.exp2(s - m), j)
-            top[g, hd] = jnp.broadcast_to(m, (half, HEAD_SIZE))
+            top[g, hd] = jnp.broadcast_to(m, (8, half))
             return carry
 
         lax.fori_loop(0, heads, one, 0, unroll=2)
@@ -141,7 +147,7 @@
         def one(hd, carry):
             cols = pl.ds(pl.multiple_of(hd * HEAD_SIZE, HEAD_SIZE), HEAD_SIZE)
             a = acc[g, hd]
-            att[g, mine, cols] = (a[:, :HEAD_SIZE] / a[:, HEAD_SIZE:]).astype(BF16)
+            att[g, mine, cols] = (a[:HEAD_SIZE] / a[HEAD_SIZE:HEAD_SIZE + 1]).T.astype(BF16)
             return carry
 
         lax.fori_loop(0, heads, one, 0)
@@ -160,6 +166,8 @@
 
     local_k.wait()
     local_v.wait()
+    turn(b)
+    local_q.wait()
     own_block(0)
     own_block(1)
 
@@ -167,6 +175,7 @@
     def _():
         for n, (buf, own) in enumerate(((kbuf, k_own), (vbuf, v_own))):
             kv_copy(buf, own, n, b - 1, partner, kv_send.at[n, nx]).wait_recv()
+        turn(b - 1)
 
     for j in range(nx - 1):
         @pl.when(j < x)
@@ -181,6 +190,8 @@
         def _():
             for n, (buf, own) in enumerate(((kbuf, k_own), (vbuf, v_own))):
                 kv_copy(buf, own, n, j * 2 + 1 - c, partner, kv_send.at[n, 0]).wait_recv()
+            turn(j * 2)
+            turn(j * 2 + 1)
 
     others(0)
     finish(0)
@@ -306,20 +317,22 @@
     return pl.pallas_call(
         functools.partial(kernel, nb, nh),
         out_shape=jax.ShapeDtypeStruct((piece, wcols * nb), BF16),
-        in_specs=[vmem, hbm, hbm, hbm],
+        in_specs=[hbm, hbm, hbm, hbm],
         out_specs=vmem,
         scratch_shapes=[
+            pltpu.VMEM((nz, 2, piece, qcols), BF16),
             pltpu.VMEM((nb, rows, HEAD_SIZE), BF16),
             pltpu.VMEM((nb, rows, HEAD_SIZE), BF16),
+            pltpu.VMEM((nb, HEAD_SIZE + TOTAL_ROWS, rows), BF16),
             pltpu.VMEM((nx, ns, depth, step), BF16),
-            pltpu.VMEM((2, heads, half, 2 * HEAD_SIZE), F32),
-            pltpu.VMEM((2, heads, half, HEAD_SIZE), F32),
+            pltpu.VMEM((2, heads, HEAD_SIZE + TOTAL_ROWS, half), F32),
+            pltpu.VMEM((2, heads, 8, half), F32),
             pltpu.VMEM((2, 2 * half, qcols), BF16),
             pltpu.VMEM((nk, 2 * half, step), BF16),
             pltpu.VMEM((nk, 2 * half, step), BF16),
             pltpu.VMEM((nk, 2 * nz, piece, step), BF16),
             pltpu.VMEM((nk, 2 * nz, piece, step), BF16),
-            dma((2 + ns,)),
+            dma((3 + ns,)),
             dma((2, nx + 1)),
             dma((2, nb)),
             dma((2, nx)),
@@ -333,7 +346,7 @@
             dma((nk, 2 * nz)),
         ],
         compiler_params=pltpu.CompilerParams(
-            collective_id=0, has_side_effects=True, vmem_limit_bytes=50 * 2**20),
+            collective_id=0, has_side_effects=True, vmem_limit_bytes=66_000_000),
     )(q, key_rows, value_head_rows, out_weight)
 
 

time: 92.8 us -> 93.2 us (level)
  Pallas kernels: 88.1 us -> 91.1 us
  local copies, waits for them, and re-layouts: 4.47 us -> 1.87 us
    pallas_call x1, Pallas kernels: 88.1 us -> 91.1 us  [shards(): pl.pallas_call(functools.partial(kernel, nb, nh), out_shape=jax.ShapeDtyp...]
    unnamed x7 -> x1, local copies, waits for them, and re-layouts: 4.47 us -> 1.87 us
where the time goes in v2:
time: 93.2 us; the launch traced here: 93 us
  Pallas kernels  91.1 us (98%)
  local copies, waits for them, and re-layouts  1.87 us (2%)
    pallas_call x1, Pallas kernels, shards(): pl.pallas_call(functools.partial(kernel, nb, nh), out_shape=jax.ShapeDtyp...  91.1 us
    unnamed x1, local copies, waits for them, and re-layouts  1.87 us

profile of v2, /device:TPU:2, one launch (start us, length us, event | category | flops | bytes accessed | tf_op | source)
XLA Modules:
  0.0 93.0 jit_solution(12538952881249336246)
XLA Ops:
  0.0 91.1 %shard_map.46 = bf16[64,4096]{1,0:T(8,128)(2,1)} custom-call(bf16[4,2,64,1024]{3,2,1,0:T(8,128)(2,1)} %bitcast.1, bf16[512,1024]{1,0:T(8,128)(2,1)} %k_ref.1, bf16[512,1024]{1,0:T(8,128)(2,1)} %v_ref.1, bf16[1024,1024]{1,0:T(8,128)(2,1)} %w_ref.1), custom_call_target="tpu_custom_call" | custom-call | tf_op jit(solution)/shard_map/pallas_call | solution.py:317
  91.2 1.9 %copy.6 = bf16[64,4096]{1,0:T(8,128)(2,1)} copy(bf16[64,4096]{1,0:T(8,128)(2,1)} %shard_map.46) | data formatting | bytes 1048576

commit v3 on v2

--- a/solution.py
+++ b/solution.py
@@ -14,12 +14,13 @@
 MASKED_SCORE = -1e30
 COLUMN_STEP = 256
 TOTAL_ROWS = 16
+KEY_TILE = 256
 F32 = jnp.float32
 BF16 = jnp.bfloat16
 
 
 def kernel(nb, nh, q_hbm, k_ref, v_ref, w_ref, out_ref,
-           q_ref, kbuf, vbuf, vturn, wbuf, acc, top, att, ysend, yrecv, zsend, zrecv,
+           q_ref, kbuf, vbuf, vturn, wbuf, sbuf, mbuf, acc, top, att, ysend, yrecv, zsend, zrecv,
            local_sem, kv_send, kv_recv, relay_send, w_send, w_recv,
            att_send, att_recv, y_send, y_recv, z_send, z_recv):
     nx, nz = nb // 2, nh // 2
@@ -99,43 +100,60 @@
     def group_y(g):
         return (1 - y) if g == 0 else y
 
-    def scores_of(g, hd, j):
-        cols = pl.ds(pl.multiple_of(hd * HEAD_SIZE, HEAD_SIZE), HEAD_SIZE)
-        q = q_ref[:, group_y(g), :, cols].reshape(half, HEAD_SIZE)
-        s = lax.dot_general(kbuf[j], q, (((1,), (1,)), ((), ())), preferred_element_type=F32)
-        return s * scale
-
     def turn(j):
         vturn[j, :HEAD_SIZE] = vbuf[j].T
         vturn[j, HEAD_SIZE:] = jnp.ones((TOTAL_ROWS, rows), BF16)
 
-    def mixed_of(p, j):
-        return jnp.dot(vturn[j], p.astype(BF16), preferred_element_type=F32)
-
-    def own_block(g):
-        row = lax.broadcasted_iota(jnp.int32, (rows, half), 1)
-        position = (row // piece * 2 + group_y(g)) * piece + row % piece
-        visible = position >= lax.broadcasted_iota(jnp.int32, (rows, half), 0)
-
-        def one(hd, carry):
-            s = jnp.where(visible, scores_of(g, hd, b), MASKED_SCORE)
-            m = jnp.max(s, axis=0, keepdims=True)
-            acc[g, hd] = mixed_of(jnp.exp2(s - m), b)
+    tile = sbuf.shape[2]
+    tiles = rows // tile
+
+    def score_tile(g, hd, j, t, own):
+        cols = pl.ds(pl.multiple_of(hd * HEAD_SIZE, HEAD_SIZE), HEAD_SIZE)
+        q = q_ref[:, group_y(g), :, cols].reshape(half, HEAD_SIZE)
+        k = kbuf[j, t * tile:(t + 1) * tile]
+        s = lax.dot_general(k, q, (((1,), (1,)), ((), ())), preferred_element_type=F32) * scale
+        if own:
+            row = lax.broadcasted_iota(jnp.int32, (tile, half), 1)
+            position = (row // piece * 2 + group_y(g)) * piece + row % piece
+            visible = position >= lax.broadcasted_iota(jnp.int32, (tile, half), 0) + t * tile
+            s = jnp.where(visible, s, MASKED_SCORE)
+        return s
+
+    def block(g, j, own):
+        def put(hd, slot, t, m):
+            s = score_tile(g, hd, j, t, own)
+            sbuf[slot, t] = s
+            n = jnp.max(s, axis=0, keepdims=True)
+            return n if m is None else jnp.maximum(m, n)
+
+        def step(hd, following, slot):
+            m = mbuf[slot][:1]
+            if not own:
+                old = top[g, hd][:1]
+                m = jnp.maximum(old, m)
+            mixed, ahead = None, None
+            for t in range(tiles):
+                ahead = put(following, 1 - slot, t, ahead)
+                p = jnp.exp2(sbuf[slot, t] - m).astype(BF16)
+                d = jnp.dot(vturn[j, :, t * tile:(t + 1) * tile], p, preferred_element_type=F32)
+                mixed = d if mixed is None else mixed + d
+            mbuf[1 - slot] = jnp.broadcast_to(ahead, (8, half))
+            if not own:
+                mixed += acc[g, hd] * jnp.exp2(old - m)
+            acc[g, hd] = mixed
             top[g, hd] = jnp.broadcast_to(m, (8, half))
-            return carry
-
-        lax.fori_loop(0, heads, one, 0, unroll=2)
-
-    def other_block(g, j):
-        def one(hd, carry):
-            s = scores_of(g, hd, j)
-            old = top[g, hd][:1]
-            m = jnp.maximum(old, jnp.max(s, axis=0, keepdims=True))
-            acc[g, hd] = acc[g, hd] * jnp.exp2(old - m) + mixed_of(jnp.exp2(s - m), j)
-            top[g, hd] = jnp.broadcast_to(m, (8, half))
-            return carry
-
-        lax.fori_loop(0, heads, one, 0, unroll=2)
+
+        ahead = None
+        for t in range(tiles):
+            ahead = put(0, 0, t, ahead)
+        mbuf[0] = jnp.broadcast_to(ahead, (8, half))
+
+        def pair(i, carry):
+            step(2 * i, 2 * i + 1, 0)
+            step(2 * i + 1, jnp.minimum(2 * i + 2, heads - 1), 1)
+            return carry
+
+        lax.fori_loop(0, heads // 2, pair, 0)
 
     mine = pl.ds(pl.multiple_of(c * half, half), half)
     theirs = pl.ds(pl.multiple_of((1 - c) * half, half), half)
@@ -156,10 +174,10 @@
     def others(g):
         @pl.when(c == 1)
         def _():
-            other_block(g, b - 1)
+            block(g, b - 1, False)
 
         def one(j, carry):
-            other_block(g, j)
+            block(g, j, False)
             return carry
 
         lax.fori_loop(0, 2 * x, one, 0)
@@ -168,8 +186,8 @@
     local_v.wait()
     turn(b)
     local_q.wait()
-    own_block(0)
-    own_block(1)
+    block(0, b, True)
+    block(1, b, True)
 
     @pl.when(c == 1)
     def _():
@@ -310,6 +328,7 @@
     step = math.gcd(wcols, COLUMN_STEP)
     ns = wcols // step
     nk = nx * ns
+    tile = math.gcd(rows, KEY_TILE)
     q = queries.reshape(nz, 2, piece, qcols)
     dma = pltpu.SemaphoreType.DMA
     vmem = pl.BlockSpec(memory_space=pltpu.VMEM)
@@ -325,6 +344,8 @@
             pltpu.VMEM((nb, rows, HEAD_SIZE), BF16),
             pltpu.VMEM((nb, HEAD_SIZE + TOTAL_ROWS, rows), BF16),
             pltpu.VMEM((nx, ns, depth, step), BF16),
+            pltpu.VMEM((2, rows // tile, tile, half), F32),
+            pltpu.VMEM((2, 8, half), F32),
             pltpu.VMEM((2, heads, HEAD_SIZE + TOTAL_ROWS, half), F32),
             pltpu.VMEM((2, heads, 8, half), F32),
             pltpu.VMEM((2, 2 * half, qcols), BF16),

time: 93.2 us -> 84.8 us (0.910)
  Pallas kernels: 91.1 us -> 82.7 us
    pallas_call x1, Pallas kernels: 91.1 us -> 82.7 us  [shards(): pl.pallas_call(functools.partial(kernel, nb, nh), out_shape=jax.ShapeDtyp...]
where the time goes in v3:
time: 84.8 us; the launch traced here: 84.6 us
  Pallas kernels  82.7 us (98%)
  local copies, waits for them, and re-layouts  1.87 us (2%)
    pallas_call x1, Pallas kernels, shards(): pl.pallas_call(functools.partial(kernel, nb, nh), out_shape=jax.ShapeDtyp...  82.7 us
    unnamed x1, local copies, waits for them, and re-layouts  1.87 us

profile of v3, /device:TPU:2, one launch (start us, length us, event | category | flops | bytes accessed | tf_op | source)
XLA Modules:
  0.0 84.6 jit_solution(13080540099194727572)
XLA Ops:
  0.0 82.7 %shard_map.46 = bf16[64,4096]{1,0:T(8,128)(2,1)} custom-call(bf16[4,2,64,1024]{3,2,1,0:T(8,128)(2,1)} %bitcast.1, bf16[512,1024]{1,0:T(8,128)(2,1)} %k_ref.1, bf16[512,1024]{1,0:T(8,128)(2,1)} %v_ref.1, bf16[1024,1024]{1,0:T(8,128)(2,1)} %w_ref.1), custom_call_target="tpu_custom_call" | custom-call | tf_op jit(solution)/shard_map/pallas_call | solution.py:336
  82.7 1.9 %copy.6 = bf16[64,4096]{1,0:T(8,128)(2,1)} copy(bf16[64,4096]{1,0:T(8,128)(2,1)} %shard_map.46) | data formatting | bytes 1048576
